TPU v7x, 256 devices: a whole 4x4x8 slice. The times are simulated.
256 devices in a mesh: req: 32 (over z, y), tp: 8 (over x, core).
Axes of the slice: x: 4, y: 4, z: 8, core: 2. Of those that a mesh axis runs over, the one named last changes fastest.
Arguments:
- attn_heads: bfloat16 [4096, 2048], P('req', 'tp'), may hold values from -6 to 6
- residual_in: bfloat16 [4096, 4096], P('req', 'tp'), may hold values from -45 to 45
- w_out: bfloat16 [2048, 4096], P('tp'), may hold values from -0.125 to 0.125
- gain_attn: float32 [4096], P('tp'), may hold values from 0.1 to 1.9
- router: bfloat16 [4096, 8], P('tp'), may hold values from -0.09375 to 0.09375
- expert_ids: int32 [4096, 2], P('req'), may hold values from 0 to 7, all different within a row; in each aligned block of 64 rows (0 to 63, 64 to 127, ...) at most 24 rows name the same one
- lengths: int32 [32, 5], P('req'), may hold values from 1 to 64, 128 in all within a row
- placement: int32 [16], replicated, may hold values from 0 to 7, as said below
- w_gate_up: bfloat16 [32, 2, 4096, 3584], P('req', None, None, 'tp'), may hold values from -1 to 1, as said below
- w_down: bfloat16 [32, 3584, 4096], P('req', 'tp'), may hold values from -1 to 1, as said below
- gain_final: float32 [4096], P('tp'), may hold values from 0.1 to 1.9
Outputs:
- residual_out: bfloat16 [4096, 4096], P('req', 'tp')
- normed_out: bfloat16 [4096, 4096], P('req', 'tp')
Inputs may be any that keep to these rules, and one draw needn't show every extreme that they name: `expert_ids`: in each aligned block of 64 rows no expert is named by more than 24 rows, and the two experts of a row differ. `placement`: every expert is held by exactly two pairs. `w_gate_up`: index 2 s + h holds the h-th half of the hidden units of expert placement[s]; the two pairs of one expert hold equal values. `w_down`: index 2 s + h holds the h-th half of the hidden units of expert placement[s]; the two pairs of one expert hold equal values.
All inputs are finite; a program needn't handle non-finite values.
Results may differ from a plain program's by a relative error of at most 0.014.
Values may be sent and summed in bfloat16 or wider, within the bound.
A program may use at most 128 MiB of HBM per device.

v0:
```python
import jax
import jax.numpy as jnp
from jax import lax
from jax.sharding import PartitionSpec as P

epsilon = 1e-05


def on_device(
    attn_heads,
    residual_in,
    w_out,
    gain_attn,
    router,
    expert_ids,
    lengths,
    placement,
    w_gate_up,
    w_down,
    gain_final,
):
    tok_rows = attn_heads.shape[0]
    half_rows = tok_rows // 2
    feat_width = residual_in.shape[1]
    full_width = feat_width * lax.axis_size("tp")
    devices = lax.axis_size("req")
    pair_count = devices // 2
    expert_count = devices // 4
    capacity = min(half_rows, 3 * tok_rows // (2 * expert_count))
    partial_out = jnp.dot(attn_heads, w_out, preferred_element_type=jnp.float32)
    state = residual_in.astype(jnp.float32) + lax.psum_scatter(
        partial_out.astype(jnp.bfloat16), "tp", scatter_dimension=1, tiled=True
    ).astype(jnp.float32)
    router_full = router.astype(jnp.float32)
    square_sum = lax.psum(jnp.sum(state * state, axis=1), "tp")
    inverse = lax.rsqrt(square_sum / full_width + epsilon)[:, None]
    normed = state * inverse * gain_attn
    logits = lax.psum(jnp.dot(normed, router_full, precision=lax.Precision.HIGHEST), "tp")
    normed_bf = normed.astype(jnp.bfloat16)
    expert_range = jnp.arange(expert_count, dtype=jnp.int32)
    match_table = expert_ids[:, :, None] == expert_range
    chosen = jnp.sum(match_table.astype(jnp.float32) * logits[:, None, :], axis=2)
    weights = jax.nn.sigmoid(chosen - chosen[:, ::-1])
    row_index = jnp.arange(tok_rows, dtype=jnp.int32)
    live_rows = row_index < tok_rows - lengths[0, lengths.shape[1] - 1]
    held_table = (placement[:, None] == expert_range).astype(jnp.int32)
    earlier = jnp.cumsum(held_table, axis=0) - held_table
    pair_range = jnp.arange(pair_count, dtype=jnp.int32)[:, None]
    first_pair = jnp.sum(pair_range * held_table * (earlier == 0).astype(jnp.int32), axis=0)
    second_pair = jnp.sum(pair_range * held_table * (earlier == 1).astype(jnp.int32), axis=0)
    upper_half = (row_index >= half_rows)[:, None, None]
    owner_table = jnp.where(upper_half, second_pair, first_pair)
    id_hot = match_table.astype(jnp.int32) * live_rows[:, None, None].astype(jnp.int32)
    target_pair = jnp.sum(id_hot * owner_table, axis=2)
    halves_hot = id_hot.reshape(2, tok_rows, expert_count)
    running = jnp.cumsum(halves_hot, axis=1) - halves_hot
    position = jnp.sum(running * halves_hot, axis=2).reshape(tok_rows, 2)
    slot_index = jnp.where(
        live_rows[:, None], target_pair * capacity + position, pair_count * capacity
    ).reshape(-1)
    source = lax.all_gather(normed_bf, "tp", axis=1, tiled=True)
    feature_dim = source.shape[1]
    sendable = jnp.zeros((pair_count * capacity + 1, feature_dim), jnp.bfloat16)
    sendable = sendable.at[slot_index].set(jnp.repeat(source, 2, axis=0))
    per_pair = sendable[: pair_count * capacity].reshape(pair_count, 1, capacity, feature_dim)
    outgoing = jnp.broadcast_to(per_pair, (pair_count, 2, capacity, feature_dim)).reshape(
        devices, capacity, feature_dim
    )
    gate_weights = w_gate_up[0, 0]
    up_weights = w_gate_up[0, 1]
    down_weights = w_down[0]
    arrived = lax.all_to_all(outgoing, "req", split_axis=0, concat_axis=0, tiled=True)
    source_count = arrived.shape[0]
    slot_count = arrived.shape[1]
    flat_rows = arrived.reshape(source_count * slot_count, full_width)
    gate_proj = jnp.dot(flat_rows, gate_weights, preferred_element_type=jnp.float32)
    up_proj = jnp.dot(flat_rows, up_weights, preferred_element_type=jnp.float32)
    activ = (jax.nn.silu(gate_proj) * up_proj).astype(jnp.bfloat16)
    down_part = jnp.dot(activ, down_weights, preferred_element_type=jnp.float32)
    reduced = lax.psum_scatter(
        down_part.astype(jnp.bfloat16), "tp", scatter_dimension=1, tiled=True
    ).astype(jnp.float32)
    returned = lax.all_to_all(
        reduced.reshape(source_count, slot_count, feat_width).astype(jnp.bfloat16),
        "req",
        split_axis=0,
        concat_axis=0,
        tiled=True,
    ).astype(jnp.float32)
    both_halves = (
        returned.reshape(pair_count, 2, capacity, feat_width)
        .sum(axis=1)
        .reshape(pair_count * capacity, feat_width)
    )
    padded = jnp.concatenate([both_halves, jnp.zeros((1, feat_width), jnp.float32)], axis=0)
    gathered_rows = padded[slot_index].reshape(tok_rows, 2, feat_width)
    mixture = gathered_rows[:, 0] * weights[:, 0:1] + gathered_rows[:, 1] * weights[:, 1:2]
    combined = state + mixture
    final_sum = lax.psum(jnp.sum(combined * combined, axis=1), "tp")
    final_scale = lax.rsqrt(final_sum / full_width + epsilon)[:, None]
    return (
        combined.astype(jnp.bfloat16),
        (combined * final_scale * gain_final).astype(jnp.bfloat16),
    )


def solution(mesh):
    placed = (
        P("req", "tp"),
        P("req", "tp"),
        P("tp", None),
        P("tp"),
        P("tp", None),
        P("req", None),
        P("req", None),
        P(),
        P("req", None, None, "tp"),
        P("req", "tp", None),
        P("tp"),
    )
    return jax.shard_map(
        on_device,
        mesh=mesh,
        in_specs=placed,
        out_specs=(P("req", "tp"), P("req", "tp")),
        check_vma=False,
    )
```

profile of v0, /device:TPU:8, one launch (start us, length us, event | category | flops | bytes accessed | tf_op | source)
XLA Modules:
  0.0 379.3 jit_solution(5766323094708515772)
XLA Ops:
  7.3 1.5 copy-done
  8.8 2.3 convolution_convert_fusion.1
  11.1 37.7 %reduce-scatter.3.cloned.1.call-done = bf16[128,512]{1,0:T(8,128)(2,1)} async-done(((bf16[128,4096]{1,0:T(8,128)(2,1)}), bf16[128,512]{1,0:T(8,128)(2,1)}) %reduce-scatter.3.cloned.1.call-update) | async-done | bytes 131088 | tf_op jit(solution)/shard_map/reduce_scatter | solution.py:31
  48.8 1.0 multiply_reduce_fusion.1
  49.8 12.9 %psum.21 = f32[128]{0:T(128)S(1)} all-reduce(f32[128]{0:T(128)S(1)} %multiply_reduce_fusion.1), channel_id=1, replica_groups=mesh['req'=32,'tp'=8] {'tp'}, use_global_device_ids=true, to_apply=%region_8.9 | all-reduce | flops 128 | bytes 1024 | tf_op jit(solution)/shard_map/psum | solution.py:35
  62.8 1.7 fusion.23
  64.5 0.6 slice.24
  66.4 0.2 reduce_window_sum.23
  67.4 0.2 fusion.24
  67.6 21.6 %all-gather.2.cloned.1.call-done = bf16[128,4096]{1,0:T(8,128)(2,1)} async-done(((bf16[128,512]{1,0:T(8,128)(2,1)}), bf16[128,4096]{1,0:T(8,128)(2,1)}) %all-gather.2.cloned.1.call-update) | async-done | bytes 1048592 | tf_op jit(solution)/shard_map/all_gather | solution.py:61
  89.3 4.7 %broadcast_in_dim.66 = bf16[128,2,4096]{2,1,0:T(2,128)(2,1)} broadcast(bf16[128,4096]{1,0:T(8,128)(2,1)} %all-gather.2.cloned.1.call-done), dimensions={0,2} | broadcast | bytes 3145728 | tf_op jit(solution)/shard_map/broadcast_in_dim | solution.py:64
  93.9 4.1 %reshape.163 = bf16[256,4096]{1,0:T(8,128)(2,1)} reshape(bf16[128,2,4096]{2,1,0:T(2,128)(2,1)} %broadcast_in_dim.66) | data formatting | bytes 4194304 | tf_op jit(solution)/shard_map/reshape | solution.py:64
  98.0 6.6 %scatter_custom_fusion = bf16[385,4096]{1,0:T(8,128)(2,1)} fusion(s32[256]{0:T(256)S(1)} %bitcast.58, bf16[256,4096]{1,0:T(8,128)(2,1)} %reshape.163, bf16[]{:T(256)} %constant.14.clone.1), kind=kCustom, calls=%fused_computation.11 | custom fusion | bytes 3154432 | tf_op jit(solution)/shard_map/scatter | solution.py:64
  104.6 1.9 slice-done
  106.5 0.8 broadcast_in_dim.68
  107.3 151.0 %all_to_all.10 = bf16[32,24,4096]{2,1,0:T(8,128)(2,1)S(1)} all-to-all(bf16[32,24,4096]{2,1,0:T(8,128)(2,1)S(1)} %bitcast.51), channel_id=1, replica_groups=mesh['req'=32,'tp'=8] {'req'}, dimensions={0} | all-to-all | bytes 12582912 | tf_op jit(solution)/shard_map/all_to_all | solution.py:72
  258.3 2.7 copy-done.1
  261.0 4.2 %fusion.3 = f32[768,448]{0,1:T(8,128)} fusion(bf16[768,4096]{1,0:T(8,128)(2,1)S(1)} %bitcast.53, bf16[1,2,4096,448]{2,3,1,0:T(8,128)(2,1)S(1)} %bitcast.61), kind=kOutput, calls=%fused_computation.7 | convolution fusion | flops 2818572288 | bytes 11337728 | tf_op jit(solution)/shard_map/dot_general | solution.py:76
  265.2 16.3 %convolution_convert_fusion = bf16[768,4096]{1,0:T(8,128)(2,1)} fusion(bf16[1,448,4096]{2,1,0:T(8,128)(2,1)} %param.20, bf16[768,4096]{1,0:T(8,128)(2,1)} %bitcast.54, bf16[1,2,4096,448]{2,3,1,0:T(8,128)(2,1)} %param.19, f32[768,448]{0,1:T(8,128)} %fusion.3), kind=kOutput, calls=%fused_computation.2 | convolution fusion | flops 5642354688 | bytes 21299200 | tf_op jit(solution)/shard_map/dot_general | solution.py:79
  281.5 40.5 %reduce-scatter.5.cloned.1.call-done = bf16[768,512]{1,0:T(8,128)(2,1)} async-done(((bf16[768,4096]{1,0:T(8,128)(2,1)}), bf16[768,512]{1,0:T(8,128)(2,1)}) %reduce-scatter.5.cloned.1.call-update) | async-done | bytes 786448 | tf_op jit(solution)/shard_map/reduce_scatter | solution.py:80
  322.0 10.2 %all-to-all-start.1 = ((bf16[32,24,512]{2,1,0:T(8,128)(2,1)}), bf16[32,24,512]{2,1,0:T(8,128)(2,1)S(1)}, u32[]{:S(2)}, u32[]{:S(2)}) async-start(bf16[32,24,512]{2,1,0:T(8,128)(2,1)} %bitcast.56), calls=%async_computation.3 | async-start | bytes 1572864 | tf_op jit(solution)/shard_map/all_to_all | solution.py:83
  332.2 0.6 pad_clamp_fusion
  332.8 0.3 fusion.22
  333.1 13.9 %psum.22 = f32[128,8]{0,1:T(8,128)S(1)} all-reduce(f32[128,8]{0,1:T(8,128)S(1)} %fusion.22), channel_id=1, replica_groups=mesh['req'=32,'tp'=8] {'tp'}, use_global_device_ids=true, to_apply=%region_12.13 | all-reduce | flops 1024 | bytes 8192 | tf_op jit(solution)/shard_map/psum | solution.py:38
  347.0 0.6 slice_bitcast_fusion.1
  347.6 6.5 %all-to-all-done.1 = bf16[32,24,512]{2,1,0:T(8,128)(2,1)S(1)} async-done(((bf16[32,24,512]{2,1,0:T(8,128)(2,1)}), bf16[32,24,512]{2,1,0:T(8,128)(2,1)S(1)}, u32[]{:S(2)}, u32[]{:S(2)}) %all-to-all-start.1) | async-done | bytes 786464 | tf_op jit(solution)/shard_map/all_to_all | solution.py:83
  354.3 1.1 gather_fusion
  355.4 0.3 reshape.148
  355.7 0.4 fusion.32
  356.1 1.1 multiply_reduce_fusion
  357.3 14.1 %psum.23 = f32[128]{0:T(128)S(1)} all-reduce(f32[128]{0:T(128)S(1)} %get-tuple-element.4), channel_id=1, replica_groups=mesh['req'=32,'tp'=8] {'tp'}, use_global_device_ids=true, to_apply=%region_15.16 | all-reduce | flops 128 | bytes 1024 | tf_op jit(solution)/shard_map/psum | solution.py:99
  371.4 1.4 multiply_convert_fusion
  (54 shorter events, 1.9 us)
Async XLA Ops:
  7.2 1.6 copy-start
  7.2 41.6 %copy-start.2 = (bf16[128,512]{1,0:T(8,128)(2,1)S(1)}, bf16[128,512]{1,0:T(8,128)(2,1)}, u32[]{:S(2)}) copy-start(bf16[128,512]{1,0:T(8,128)(2,1)} %param.12) | copy-start | bytes 393220
  7.2 55.6 %copy-start.5 = (f32[512]{0:T(512)S(1)}, f32[512]{0:T(512)}, u32[]{:S(2)}) copy-start(f32[512]{0:T(512)} %param.14) | copy-start | bytes 6148
  7.2 57.3 %copy-start.8 = (s32[1,5]{1,0:T(1,128)S(1)}, s32[1,5]{1,0:T(1,128)}, u32[]{:S(2)}) copy-start(s32[1,5]{1,0:T(1,128)} %param.17) | copy-start | bytes 64
  7.2 58.8 %copy-start.4 = (s32[128,2]{0,1:T(2,128)S(1)}, s32[128,2]{0,1:T(2,128)}, u32[]{:S(2)}) copy-start(s32[128,2]{0,1:T(2,128)} %param.16) | copy-start | bytes 3076
  7.2 59.4 %copy-start.6 = (s32[16]{0:T(128)S(1)}, s32[16]{0:T(128)}, u32[]{:S(2)}) copy-start(s32[16]{0:T(128)} %param.18) | copy-start | bytes 196
  7.2 41.6 %reduce-scatter.3.cloned.1.call-start = ((), (), s32[]{:S(2)}) async-start(), calls=%async_computation.4 | async-start | bytes 1179648 | tf_op jit(solution)/shard_map/reduce_scatter | solution.py:31
  11.1 78.2 %all-gather.2.cloned.1.call-start = ((), (), s32[]{:S(2)}) async-start(), calls=%async_computation.5 | async-start | bytes 1179648 | tf_op jit(solution)/shard_map/all_gather | solution.py:61
  64.4 257.6 %reduce-scatter.5.cloned.1.call-start = ((), (), s32[]{:S(2)}) async-start(), calls=%async_computation.6 | async-start | bytes 7077888 | tf_op jit(solution)/shard_map/reduce_scatter | solution.py:80
  104.6 1.9 slice-start
  106.5 154.5 %slice-start.1 = ((s8[7340032]{0:T(1024)(128)(4,1)}), s8[3145728]{0:T(1024)(128)(4,1)S(1)}, s32[]{:S(2)}) async-start(s8[7340032]{0:T(1024)(128)(4,1)} %bitcast.60), calls=%async_computation.8 | async-start | bytes 6291456
  107.3 153.7 %slice-start.2 = ((s8[7340032]{0:T(1024)(128)(4,1)}), s8[4194304]{0:T(1024)(128)(4,1)S(1)}, s32[]{:S(2)}) async-start(s8[7340032]{0:T(1024)(128)(4,1)} %bitcast.60), calls=%async_computation.9 | async-start | bytes 8388608
  258.3 2.7 copy-start.1
  281.5 51.3 %copy-start.3 = (bf16[128,512]{1,0:T(8,128)(2,1)S(1)}, bf16[128,512]{1,0:T(8,128)(2,1)}, u32[]{:S(2)}) copy-start(bf16[128,512]{1,0:T(8,128)(2,1)} %reduce-scatter.3.cloned.1.call-done) | copy-start | bytes 393220
  281.5 51.3 %copy-start.7 = (bf16[512,8]{0,1:T(8,128)(2,1)S(1)}, bf16[512,8]{0,1:T(8,128)(2,1)}, u32[]{:S(2)}) copy-start(bf16[512,8]{0,1:T(8,128)(2,1)} %param.15) | copy-start | bytes 24580
  322.0 32.1 %all-to-all-start.1 = ((bf16[32,24,512]{2,1,0:T(8,128)(2,1)}), bf16[32,24,512]{2,1,0:T(8,128)(2,1)S(1)}, u32[]{:S(2)}, u32[]{:S(2)}) async-start(bf16[32,24,512]{2,1,0:T(8,128)(2,1)} %bitcast.56), calls=%async_computation.3 | async-start | bytes 1572864 | tf_op jit(solution)/shard_map/all_to_all | solution.py:83
Sparse Core Ops, SparseCore 0:
  11.2 37.5 reduce-scatter.2
  64.6 24.6 all-gather.1
  281.7 40.3 reduce-scatter.4
where the time goes:
time: 380 us; the launch traced here: 379 us
  blocking collectives  192 us (51%)
  waiting for transfers between devices  106 us (28%)
  local copies, waits for them, and re-layouts  26.3 us (7%)
  matrix products  23.1 us (6%)
  between operations  14.6 us (4%)
  starting transfers between devices  10.3 us (3%)
  other arithmetic  6.89 us (2%)
    all_to_all x1, blocking collectives, on_device(): lax.all_to_all(outgoing, 'req', split_axis=0, concat_axis=0, tiled=True)  151 us
    reduce_scatter x1, waiting for transfers between devices, on_device(): lax.psum_scatter(down_part.astype(jnp.bfloat16), 'tp', scatter_dimension=...  40.5 us
    reduce_scatter x1, waiting for transfers between devices, on_device(): lax.psum_scatter(partial_out.astype(jnp.bfloat16), 'tp', scatter_dimensio...  37.7 us
    all_gather x1, waiting for transfers between devices, on_device(): source = lax.all_gather(normed_bf, 'tp', axis=1, tiled=True)  21.6 us
    dot_general x1, matrix products, on_device(): down_part = jnp.dot(activ, down_weights, preferred_element_type=jnp.float32)  16.3 us
    psum x1, blocking collectives, on_device(): final_sum = lax.psum(jnp.sum(combined * combined, axis=1), 'tp')  14.1 us
    psum x1, blocking collectives, on_device(): lax.psum(jnp.dot(normed, router_full, precision=lax.Precision.HIGHEST), '...  13.9 us
    psum x1, blocking collectives, on_device(): square_sum = lax.psum(jnp.sum(state * state, axis=1), 'tp')  12.9 us
  transfers between devices with their start and end apart: 4, of which 4 were waited for; matrix products, arithmetic and copies ran while one was open for 1% of the time, Pallas kernels for 0%

commit v1 on v0

--- a/solution.py
+++ b/solution.py
@@ -58,7 +58,9 @@
     slot_index = jnp.where(
         live_rows[:, None], target_pair * capacity + position, pair_count * capacity
     ).reshape(-1)
-    source = lax.all_gather(normed_bf, "tp", axis=1, tiled=True)
+    source = jnp.concatenate(
+        lax.all_to_all(jnp.stack([normed_bf] * lax.axis_size("tp")), "tp", 0, 0), axis=1
+    )
     feature_dim = source.shape[1]
     sendable = jnp.zeros((pair_count * capacity + 1, feature_dim), jnp.bfloat16)
     sendable = sendable.at[slot_index].set(jnp.repeat(source, 2, axis=0))

time: 380 us -> 376 us (0.989)
  waiting for transfers between devices: 106 us -> 93.3 us
  local copies, waits for them, and re-layouts: 26.3 us -> 30.1 us
    all_gather x1 -> x0, waiting for transfers between devices: 21.6 us -> none  [on_device(): source = lax.all_gather(normed_bf, 'tp', axis=1, tiled=True)]
    all_to_all x0 -> x1, waiting for transfers between devices: none -> 12.3 us  [on_device(): lax.all_to_all(jnp.stack([normed_bf] * lax.axis_size('tp')), 'tp', 0, 0)]
  transfers between devices with their start and end apart: 4 -> 4, of which waited for: 4 -> 4; matrix products, arithmetic and copies ran while one was open for 1% -> 2% of each run, Pallas kernels for 0% -> 0%
where the time goes in v1:
time: 376 us
  blocking collectives  191 us (51%)
  waiting for transfers between devices  93.3 us (25%)
  local copies, waits for them, and re-layouts  30.1 us (8%)
  matrix products  23.1 us (6%)
  between operations  14.9 us (4%)
  starting transfers between devices  13.8 us (4%)
  other arithmetic  9.19 us (2%)
    all_to_all x1, blocking collectives, on_device(): lax.all_to_all(outgoing, 'req', split_axis=0, concat_axis=0, tiled=True)  150 us
    reduce_scatter x1, waiting for transfers between devices, on_device(): lax.psum_scatter(down_part.astype(jnp.bfloat16), 'tp', scatter_dimension=...  40.1 us
    reduce_scatter x1, waiting for transfers between devices, on_device(): lax.psum_scatter(partial_out.astype(jnp.bfloat16), 'tp', scatter_dimensio...  34.5 us
    dot_general x1, matrix products, on_device(): down_part = jnp.dot(activ, down_weights, preferred_element_type=jnp.float32)  16.3 us
    psum x1, blocking collectives, on_device(): final_sum = lax.psum(jnp.sum(combined * combined, axis=1), 'tp')  14.1 us
    psum x1, blocking collectives, on_device(): lax.psum(jnp.dot(normed, router_full, precision=lax.Precision.HIGHEST), '...  13.9 us
    psum x1, blocking collectives, on_device(): square_sum = lax.psum(jnp.sum(state * state, axis=1), 'tp')  12.9 us
    all_to_all x1, waiting for transfers between devices, on_device(): lax.all_to_all(jnp.stack([normed_bf] * lax.axis_size('tp')), 'tp', 0, 0)  12.3 us
  transfers between devices with their start and end apart: 4, of which 4 were waited for; matrix products, arithmetic and copies ran while one was open for 2% of the time, Pallas kernels for 0%

profile of v1, /device:TPU:8, one launch (start us, length us, event | category | flops | bytes accessed | tf_op | source)
XLA Modules:
  0.0 375.7 jit_solution(1695460836093451233)
XLA Ops:
  7.3 1.5 copy-done
  8.8 2.3 convolution_convert_fusion.1
  13.5 0.6 select_reduce_fusion.2
  14.3 34.5 %reduce-scatter.3.cloned.1.call-done = bf16[128,512]{1,0:T(8,128)(2,1)} async-done(((bf16[128,4096]{1,0:T(8,128)(2,1)}), bf16[128,512]{1,0:T(8,128)(2,1)}) %reduce-scatter.3.cloned.1.call-update) | async-done | bytes 131088 | tf_op jit(solution)/shard_map/reduce_scatter | solution.py:31
  48.8 1.0 multiply_reduce_fusion.1
  49.8 12.9 %psum.21 = f32[128]{0:T(128)S(1)} all-reduce(f32[128]{0:T(128)S(1)} %multiply_reduce_fusion.1), channel_id=1, replica_groups=mesh['req'=32,'tp'=8] {'tp'}, use_global_device_ids=true, to_apply=%region_8.9 | all-reduce | flops 128 | bytes 1024 | tf_op jit(solution)/shard_map/psum | solution.py:35
  63.3 1.0 fusion.23
  64.3 1.1 stack.2
  65.4 3.6 all-to-all-start
  69.8 0.7 broadcast_select_fusion
  70.5 0.6 multiply_reduce_fusion.2
  71.4 0.8 broadcast_in_dim.60
  72.5 12.3 %all-to-all-done = bf16[8,128,512]{2,1,0:T(8,128)(2,1)S(1)} async-done(((bf16[8,128,512]{2,1,0:T(8,128)(2,1)}), bf16[8,128,512]{2,1,0:T(8,128)(2,1)S(1)}, u32[]{:S(2)}, u32[]{:S(2)}) %all-to-all-start) | async-done | bytes 1048608 | tf_op jit(solution)/shard_map/all_to_all | solution.py:62
  84.8 1.3 copy.34
  86.1 1.5 copy.35
  87.6 3.5 broadcast_in_dim.66
  91.1 4.1 %reshape.173 = bf16[256,4096]{1,0:T(8,128)(2,1)} reshape(bf16[128,2,4096]{2,1,0:T(2,128)(2,1)} %broadcast_in_dim.66) | data formatting | bytes 4194304 | tf_op jit(solution)/shard_map/reshape | solution.py:66
  95.2 6.6 %scatter_custom_fusion = bf16[385,4096]{1,0:T(8,128)(2,1)} fusion(s32[256]{0:T(256)S(1)} %bitcast.62, bf16[256,4096]{1,0:T(8,128)(2,1)} %reshape.173, bf16[]{:T(256)} %constant.14.clone.1), kind=kCustom, calls=%fused_computation.11 | custom fusion | bytes 3154432 | tf_op jit(solution)/shard_map/scatter | solution.py:66
  101.7 1.9 slice-done
  103.6 0.8 broadcast_in_dim.68
  104.4 150.4 %all_to_all.15 = bf16[32,24,4096]{2,1,0:T(8,128)(2,1)S(1)} all-to-all(bf16[32,24,4096]{2,1,0:T(8,128)(2,1)S(1)} %bitcast.54), channel_id=1, replica_groups=mesh['req'=32,'tp'=8] {'req'}, dimensions={0} | all-to-all | bytes 12582912 | tf_op jit(solution)/shard_map/all_to_all | solution.py:74
  254.8 2.7 copy-done.1
  257.5 4.2 %fusion.3 = f32[768,448]{0,1:T(8,128)} fusion(bf16[768,4096]{1,0:T(8,128)(2,1)S(1)} %bitcast.56, bf16[1,2,4096,448]{2,3,1,0:T(8,128)(2,1)S(1)} %bitcast.65), kind=kOutput, calls=%fused_computation.7 | convolution fusion | flops 2818572288 | bytes 11337728 | tf_op jit(solution)/shard_map/dot_general | solution.py:78
  261.7 16.3 %convolution_convert_fusion = bf16[768,4096]{1,0:T(8,128)(2,1)} fusion(bf16[1,448,4096]{2,1,0:T(8,128)(2,1)} %param.20, bf16[768,4096]{1,0:T(8,128)(2,1)} %bitcast.57, bf16[1,2,4096,448]{2,3,1,0:T(8,128)(2,1)} %param.19, f32[768,448]{0,1:T(8,128)} %fusion.3), kind=kOutput, calls=%fused_computation.2 | convolution fusion | flops 5642354688 | bytes 21299200 | tf_op jit(solution)/shard_map/dot_general | solution.py:81
  278.0 40.1 %reduce-scatter.5.cloned.1.call-done = bf16[768,512]{1,0:T(8,128)(2,1)} async-done(((bf16[768,4096]{1,0:T(8,128)(2,1)}), bf16[768,512]{1,0:T(8,128)(2,1)}) %reduce-scatter.5.cloned.1.call-update) | async-done | bytes 786448 | tf_op jit(solution)/shard_map/reduce_scatter | solution.py:82
  318.1 10.2 %all-to-all-start.2 = ((bf16[32,24,512]{2,1,0:T(8,128)(2,1)}), bf16[32,24,512]{2,1,0:T(8,128)(2,1)S(1)}, u32[]{:S(2)}, u32[]{:S(2)}) async-start(bf16[32,24,512]{2,1,0:T(8,128)(2,1)} %bitcast.60), calls=%async_computation.4 | async-start | bytes 1572864 | tf_op jit(solution)/shard_map/all_to_all | solution.py:85
  329.1 13.9 %psum.22 = f32[128,8]{0,1:T(8,128)S(1)} all-reduce(f32[128,8]{0,1:T(8,128)S(1)} %fusion.22), channel_id=1, replica_groups=mesh['req'=32,'tp'=8] {'tp'}, use_global_device_ids=true, to_apply=%region_12.13 | all-reduce | flops 1024 | bytes 8192 | tf_op jit(solution)/shard_map/psum | solution.py:38
  343.7 6.5 %all-to-all-done.2 = bf16[32,24,512]{2,1,0:T(8,128)(2,1)S(1)} async-done(((bf16[32,24,512]{2,1,0:T(8,128)(2,1)}), bf16[32,24,512]{2,1,0:T(8,128)(2,1)S(1)}, u32[]{:S(2)}, u32[]{:S(2)}) %all-to-all-start.2) | async-done | bytes 786464 | tf_op jit(solution)/shard_map/all_to_all | solution.py:85
  350.4 1.1 gather_fusion
  352.2 1.1 multiply_reduce_fusion
  353.3 14.1 %psum.23 = f32[128]{0:T(128)S(1)} all-reduce(f32[128]{0:T(128)S(1)} %get-tuple-element.4), channel_id=1, replica_groups=mesh['req'=32,'tp'=8] {'tp'}, use_global_device_ids=true, to_apply=%region_15.16 | all-reduce | flops 128 | bytes 1024 | tf_op jit(solution)/shard_map/psum | solution.py:101
  367.4 1.4 multiply_convert_fusion
  (64 shorter events, 6.5 us)
Async XLA Ops:
  7.2 1.6 copy-start
  7.2 3.9 %copy-start.12 = (s32[1,5]{1,0:T(1,128)S(1)}, s32[1,5]{1,0:T(1,128)}, u32[]{:S(2)}) copy-start(s32[1,5]{1,0:T(1,128)} %param.17) | copy-start | bytes 64
  7.2 5.4 %copy-start.4 = (s32[128,2]{0,1:T(2,128)S(1)}, s32[128,2]{0,1:T(2,128)}, u32[]{:S(2)}) copy-start(s32[128,2]{0,1:T(2,128)} %param.16) | copy-start | bytes 3076
  7.2 5.6 %copy-start.7 = (s32[16]{0:T(128)S(1)}, s32[16]{0:T(128)}, u32[]{:S(2)}) copy-start(s32[16]{0:T(128)} %param.18) | copy-start | bytes 196
  7.2 41.6 %copy-start.2 = (bf16[128,512]{1,0:T(8,128)(2,1)S(1)}, bf16[128,512]{1,0:T(8,128)(2,1)}, u32[]{:S(2)}) copy-start(bf16[128,512]{1,0:T(8,128)(2,1)} %param.12) | copy-start | bytes 393220
  7.2 56.1 %copy-start.5 = (f32[512]{0:T(512)S(1)}, f32[512]{0:T(512)}, u32[]{:S(2)}) copy-start(f32[512]{0:T(512)} %param.14) | copy-start | bytes 6148
  7.2 41.6 %reduce-scatter.3.cloned.1.call-start = ((), (), s32[]{:S(2)}) async-start(), calls=%async_computation.5 | async-start | bytes 1179648 | tf_op jit(solution)/shard_map/reduce_scatter | solution.py:31
  62.8 0.5 copy-start.9
  64.3 5.5 %copy-start.8 = (s32[8]{0:T(128)S(1)}, s32[8]{0:T(128)}, u32[]{:S(2)}) copy-start(s32[8]{0:T(128)} %get-tuple-element.2) | copy-start | bytes 100
  65.4 19.4 %all-to-all-start = ((bf16[8,128,512]{2,1,0:T(8,128)(2,1)}), bf16[8,128,512]{2,1,0:T(8,128)(2,1)S(1)}, u32[]{:S(2)}, u32[]{:S(2)}) async-start(bf16[8,128,512]{2,1,0:T(8,128)(2,1)} %stack.2), calls=%async_computation.1 | async-start | bytes 2097152 | tf_op jit(solution)/shard_map/all_to_all | solution.py:62
  68.9 249.1 %reduce-scatter.5.cloned.1.call-start = ((), (), s32[]{:S(2)}) async-start(), calls=%async_computation.6 | async-start | bytes 7077888 | tf_op jit(solution)/shard_map/reduce_scatter | solution.py:82
  101.7 1.9 slice-start
  103.6 153.8 %slice-start.1 = ((s8[7340032]{0:T(1024)(128)(4,1)}), s8[3145728]{0:T(1024)(128)(4,1)S(1)}, s32[]{:S(2)}) async-start(s8[7340032]{0:T(1024)(128)(4,1)} %bitcast.64), calls=%async_computation.8 | async-start | bytes 6291456
  104.4 153.0 %slice-start.2 = ((s8[7340032]{0:T(1024)(128)(4,1)}), s8[4194304]{0:T(1024)(128)(4,1)S(1)}, s32[]{:S(2)}) async-start(s8[7340032]{0:T(1024)(128)(4,1)} %bitcast.64), calls=%async_computation.9 | async-start | bytes 8388608
  254.8 2.7 copy-start.1
  278.0 50.9 %copy-start.3 = (bf16[128,512]{1,0:T(8,128)(2,1)S(1)}, bf16[128,512]{1,0:T(8,128)(2,1)}, u32[]{:S(2)}) copy-start(bf16[128,512]{1,0:T(8,128)(2,1)} %reduce-scatter.3.cloned.1.call-done) | copy-start | bytes 393220
  278.0 50.9 %copy-start.6 = (f32[512]{0:T(512)S(1)}, f32[512]{0:T(512)}, u32[]{:S(2)}) copy-start(f32[512]{0:T(512)} %param.14) | copy-start | bytes 6148
  278.0 50.9 %copy-start.10 = (f32[128]{0:T(128)S(1)}, f32[128]{0:T(128)}, u32[]{:S(2)}) copy-start(f32[128]{0:T(128)} %copy-done.9) | copy-start | bytes 1540
  278.0 50.9 %copy-start.11 = (bf16[512,8]{0,1:T(8,128)(2,1)S(1)}, bf16[512,8]{0,1:T(8,128)(2,1)}, u32[]{:S(2)}) copy-start(bf16[512,8]{0,1:T(8,128)(2,1)} %param.15) | copy-start | bytes 24580
  318.1 32.1 %all-to-all-start.2 = ((bf16[32,24,512]{2,1,0:T(8,128)(2,1)}), bf16[32,24,512]{2,1,0:T(8,128)(2,1)S(1)}, u32[]{:S(2)}, u32[]{:S(2)}) async-start(bf16[32,24,512]{2,1,0:T(8,128)(2,1)} %bitcast.60), calls=%async_computation.4 | async-start | bytes 1572864 | tf_op jit(solution)/shard_map/all_to_all | solution.py:85
Sparse Core Ops, SparseCore 0:
  11.2 37.5 reduce-scatter.2
  278.1 39.8 reduce-scatter.4
